TPU v7x, 32 devices: a whole 2x2x4 slice. The times are simulated.
32 devices in a mesh: rows: 16 (over z, x, core), cols: 2 (over y).
Axes of the slice: x: 2, y: 2, z: 4, core: 2. Of those that a mesh axis runs over, the one named last changes fastest.
Arguments:
- kernel: float32 [16384, 1536], P('rows', 'cols'), may hold values from -0.15625 to 0.15625
- row_orbitals: float32 [16384, 512], P('rows', 'cols'), may hold values from -1.5 to 1.5
- col_orbitals: float32 [1536, 512], P('cols', 'rows'), may hold values from -1.5 to 1.5
- col_vectors: float32 [1536, 512], P('cols', 'rows'), may hold values from -6 to 6
Outputs:
- exchange: float32 [512, 16384], P('cols', 'rows')
All inputs are finite; a program needn't handle non-finite values.
Results may differ from a plain program's by a relative error of at most 0.0003.
Values sent between devices are 32-bit elements; how exact they have to be, the bound alone decides.
A program may use at most 64 MiB of HBM per device.

v0:
```python
import functools

import jax
import jax.numpy as jnp
from jax import lax
from jax.experimental import pallas as pl
from jax.experimental.pallas import tpu as pltpu
from jax.sharding import PartitionSpec as P

MESH = pl.DeviceIdType.MESH
LEFT, RIGHT, PAIR, CORE = range(4)


def split(x):
    hi = x.astype(jnp.bfloat16)
    return hi, (x - hi.astype(jnp.float32)).astype(jnp.bfloat16)


def dot3(a_hi, a_lo, b_hi, b_lo, dims):
    dot = functools.partial(lax.dot_general, dimension_numbers=(dims, ((), ())), preferred_element_type=jnp.float32)
    return dot(a_lo, b_hi) + dot(a_hi, b_lo) + dot(a_hi, b_hi)


def exchange_kernel(
    nr, nc, chunks,
    k_hbm, row_hbm, orb_hbm, vec_hbm, out_ref,
    k, rows, orb, vec, orb_hi, orb_lo, vec_hi, vec_lo, theirs, got, mine,
    local_sem, row_send, row_recv, col_send, col_recv, core_recv, out_send, out_recv,
):
    r, c = lax.axis_index("rows"), lax.axis_index("cols")
    core, chip = lax.rem(r, 2), r // 2
    pair, line, lines = lax.rem(chip, 2), chip // 2, nr // 4
    per = orb_hbm.shape[0]
    chunk = row_hbm.shape[0] // chunks
    mb = row_hbm.shape[1]
    nb = theirs.shape[2]

    def at(l, p, q):
        return (l * 2 + p) * 2 + q

    goal = {
        LEFT: at(line - 1, pair, core),
        RIGHT: at(line + 1, pair, core),
        PAIR: at(line, 1 - pair, core),
        CORE: at(line, pair, 1 - core),
    }
    has_left, has_right = line > 0, line < lines - 1

    barrier = pltpu.get_barrier_semaphore()

    def greet(row, col):
        pl.semaphore_signal(barrier, inc=1, device_id=(row, col), device_id_type=MESH)

    for j in range(1, nc):
        greet(r, lax.rem(c + j, nc))
    greet(goal[PAIR], c)
    greet(goal[CORE], c)
    pl.when(has_left)(lambda: greet(goal[LEFT], c))
    pl.when(has_right)(lambda: greet(goal[RIGHT], c))

    k_copy = pltpu.make_async_copy(k_hbm, k, local_sem.at[0])
    row_copy = pltpu.make_async_copy(row_hbm, rows.at[0], local_sem.at[1])
    own = pl.ds(pl.multiple_of(r * per, per), per)
    orb_copy = pltpu.make_async_copy(orb_hbm, orb.at[own], local_sem.at[2])
    vec_copy = pltpu.make_async_copy(vec_hbm, vec.at[own], local_sem.at[3])
    for copy in (k_copy, row_copy, orb_copy, vec_copy):
        copy.start()

    pl.semaphore_wait(barrier, nc - 1 + 2 + has_left.astype(jnp.int32) + has_right.astype(jnp.int32))

    def row_chunk(j, i):
        at_rows = pl.ds(i * chunk, chunk) if isinstance(i, int) else pl.ds(pl.multiple_of(i * chunk, chunk), chunk)
        return pltpu.make_async_remote_copy(
            src_ref=row_hbm.at[at_rows],
            dst_ref=rows.at[j, at_rows],
            send_sem=row_send.at[j - 1],
            recv_sem=row_recv.at[j - 1, i],
            device_id=(r, lax.rem(c + j, nc)),
            device_id_type=MESH,
        )

    for i in range(chunks):
        for j in range(1, nc):
            row_chunk(j, i).start()

    def shard(t, l, p, way, first=False):
        there = (orb, vec)[t].at[pl.ds(pl.multiple_of(at(l, p, core) * per, per), per)]
        return pltpu.make_async_remote_copy(
            src_ref=(orb_hbm, vec_hbm)[t] if first else there,
            dst_ref=there,
            send_sem=col_send.at[way],
            recv_sem=core_recv.at[0] if way == CORE else col_recv.at[t, p, l],
            device_id=(goal[way], c),
            device_id_type=MESH,
        )

    def line_sources(d):
        if d == 0:
            return [(line, None, ((LEFT, has_left), (RIGHT, has_right), (PAIR, None), (CORE, None)))]
        return [
            (line - d, line - d >= 0, ((RIGHT, has_right), (PAIR, None), (CORE, None))),
            (line + d, line + d < lines, ((LEFT, has_left), (PAIR, None), (CORE, None))),
        ]

    def when(cond, do):
        if cond is None:
            do()
        else:
            pl.when(cond)(do)

    def keep(t, s):
        here = pl.ds(pl.multiple_of(s * per, per), per)
        if t == 0:
            orb_hi[here], orb_lo[here] = split(orb[here])
        else:
            vec_hi[here], vec_lo[here] = split(-vec[here])

    def pass_on(t, d):
        for l, there, ways in line_sources(d):
            def go(l=l, ways=ways):
                if d > 0:
                    shard(t, l, pair, PAIR).wait_recv()
                for way, cond in ways:
                    when(cond, shard(t, l, pair, way, d == 0).start)
                if d > 0:
                    keep(t, at(l, pair, core))
            when(there, go)

    def pass_over(t, d):
        for l, there, _ in line_sources(d):
            def go(l=l):
                shard(t, l, 1 - pair, PAIR).wait_recv()
                shard(t, l, 1 - pair, CORE).start()
                keep(t, at(l, 1 - pair, core))
            when(there, go)

    for d in range(lines):
        for t in range(2):
            pass_on(t, d)
        if d > 0:
            for t in range(2):
                pass_over(t, d - 1)
    for t in range(2):
        pass_over(t, lines - 1)

    def bulk(way, count):
        part = orb.at[pl.ds(0, count * per)]
        return pltpu.make_async_remote_copy(
            src_ref=part,
            dst_ref=part,
            send_sem=col_send.at[way],
            recv_sem=core_recv.at[0],
            device_id=(goal[CORE], c),
            device_id_type=MESH,
        )

    for copy in (orb_copy, vec_copy, k_copy, row_copy):
        copy.wait()
    for t in range(2):
        keep(t, r)
    bulk(CORE, nr).wait_recv()
    for t in range(2):

        @pl.loop(0, nr // 2)
        def _(m, t=t):
            keep(t, m * 2 + 1 - core)

    def out_chunk(j, i):
        return pltpu.make_async_remote_copy(
            src_ref=theirs.at[j - 1, i],
            dst_ref=got.at[j - 1, i],
            send_sem=out_send.at[j - 1],
            recv_sem=out_recv.at[j - 1, i],
            device_id=(r, lax.rem(c + j, nc)),
            device_id_type=MESH,
        )

    @pl.loop(0, chunks)
    def _(i):
        here = pl.ds(pl.multiple_of(i * chunk, chunk), chunk)
        gram = None
        for j in range(nc):
            if j > 0:
                row_chunk(j, i).wait_recv()
            block = pl.ds(pl.multiple_of(lax.rem(c - j + nc, nc) * mb, mb), mb)
            term = dot3(*split(rows[j, here, :]), orb_hi[block], orb_lo[block], ((1,), (0,)))
            gram = term if gram is None else gram + term
        w_hi, w_lo = split(k[here] * gram)
        for j in list(range(1, nc)) + [0]:
            block = pl.ds(pl.multiple_of(lax.rem(c + j, nc) * nb, nb), nb)
            part = dot3(vec_hi[block], vec_lo[block], w_hi, w_lo, ((1,), (1,)))
            if j == 0:
                mine[i] = part
            else:
                theirs[j - 1, i] = part
                out_chunk(j, i).start()

    bulk(PAIR, 2 * lines).wait_send()
    bulk(CORE, nr).wait_send()
    for l in range(lines):
        if l > 0:
            pl.when(line == l)(bulk(LEFT, 2 * (lines - l)).wait_send)
        if l < lines - 1:
            pl.when(line == l)(bulk(RIGHT, 2 * (l + 1)).wait_send)

    for i in range(chunks):
        total = mine[i]
        for j in range(1, nc):
            out_chunk(j, i).wait_recv()
            total = total + got[j - 1, i]
        out_ref[:, i * chunk:(i + 1) * chunk] = total
    for j in range(1, nc):
        peer = {"device_id": (r, lax.rem(c + j, nc)), "device_id_type": MESH}
        pltpu.make_async_remote_copy(
            row_hbm, rows.at[j], row_send.at[j - 1], row_recv.at[j - 1, 0], **peer
        ).wait_send()
        pltpu.make_async_remote_copy(
            theirs.at[j - 1], got.at[j - 1], out_send.at[j - 1], out_recv.at[j - 1, 0], **peer
        ).wait_send()


def solution(mesh):
    nr, nc = mesh.shape["rows"], mesh.shape["cols"]

    def body(kernel, row_orbitals, col_orbitals, col_vectors):
        n_rows, n_cols = kernel.shape
        mb, per = row_orbitals.shape[1], col_orbitals.shape[1]
        norb = mb * nc
        nb = norb // nc
        chunks = n_rows // 256
        chunk = n_rows // chunks
        f32, bf16, dma = jnp.float32, jnp.bfloat16, pltpu.SemaphoreType.DMA
        return pl.pallas_call(
            functools.partial(exchange_kernel, nr, nc, chunks),
            out_shape=pltpu.VMEM((nb, n_rows), f32),
            in_specs=[pl.BlockSpec(memory_space=pl.ANY)] * 4,
            out_specs=pl.BlockSpec(memory_space=pltpu.VMEM),
            scratch_shapes=[
                pltpu.VMEM((n_rows, n_cols), f32),
                pltpu.VMEM((nc, n_rows, mb), f32),
                pltpu.VMEM((norb, n_cols), f32),
                pltpu.VMEM((norb, n_cols), f32),
                pltpu.VMEM((norb, n_cols), bf16),
                pltpu.VMEM((norb, n_cols), bf16),
                pltpu.VMEM((norb, n_cols), bf16),
                pltpu.VMEM((norb, n_cols), bf16),
                pltpu.VMEM((nc - 1, chunks, nb, chunk), f32),
                pltpu.VMEM((nc - 1, chunks, nb, chunk), f32),
                pltpu.VMEM((chunks, nb, chunk), f32),
                dma((4,)),
                dma((nc - 1,)),
                dma((nc - 1, chunks)),
                dma((4,)),
                dma((2, 2, nr // 4)),
                dma((1,)),
                dma((nc - 1,)),
                dma((nc - 1, chunks)),
            ],
            compiler_params=pltpu.CompilerParams(
                collective_id=0, has_side_effects=True, vmem_limit_bytes=60 * 1024 * 1024
            ),
        )(kernel, row_orbitals, col_orbitals.T, col_vectors.T)

    in_specs = (P("rows", "cols"), P("rows", "cols"), P("cols", "rows"), P("cols", "rows"))
    out_specs = P("cols", "rows")
    return jax.shard_map(body, mesh=mesh, in_specs=in_specs, out_specs=out_specs, check_vma=False)
```

profile of v0, /device:TPU:0, one launch (start us, length us, event | category | flops | bytes accessed | tf_op | source)
XLA Modules:
  0.0 50.9 jit_solution(9876069361055306659)
XLA Ops:
  0.0 49.9 %shard_map.46 = f32[256,1024]{1,0:T(8,128)S(1)} custom-call(f32[1024,768]{1,0:T(8,128)} %k_hbm.1, f32[1024,256]{1,0:T(8,128)} %row_hbm.1, f32[32,768]{1,0:T(8,128)} %bitcast.2, f32[32,768]{1,0:T(8,128)} %bitcast.3), custom_call_target="tpu_custom_call" | custom-call | tf_op jit(solution)/shard_map/pallas_call | solution.py:233
  49.9 1.0 %copy.6 = f32[256,1024]{1,0:T(8,128)} copy(f32[256,1024]{1,0:T(8,128)S(1)} %shard_map.46) | data formatting | bytes 2097152
where the time goes:
time: 51.1 us; the launch traced here: 50.9 us
  Pallas kernels  49.9 us (98%)
  local copies, waits for them, and re-layouts  0.97 us (2%)
    pallas_call x1, Pallas kernels, body(): pl.pallas_call(functools.partial(exchange_kernel, nr, nc, chunks), out_sh...  49.9 us

commit v1 on v0

--- a/solution.py
+++ b/solution.py
@@ -25,7 +25,7 @@
     nr, nc, chunks,
     k_hbm, row_hbm, orb_hbm, vec_hbm, out_ref,
     k, rows, orb, vec, orb_hi, orb_lo, vec_hi, vec_lo, theirs, got, mine,
-    local_sem, row_send, row_recv, col_send, col_recv, core_recv, out_send, out_recv,
+    local_sem, ready, row_send, row_recv, col_send, col_recv, core_recv, out_send, out_recv,
 ):
     r, c = lax.axis_index("rows"), lax.axis_index("cols")
     core, chip = lax.rem(r, 2), r // 2
@@ -53,9 +53,8 @@
 
     for j in range(1, nc):
         greet(r, lax.rem(c + j, nc))
-    greet(goal[PAIR], c)
-    greet(goal[CORE], c)
-    pl.when(has_left)(lambda: greet(goal[LEFT], c))
+    pl.when(core == 1)(lambda: greet(goal[CORE], c))
+    pl.when(pair == 0)(lambda: greet(goal[PAIR], c))
     pl.when(has_right)(lambda: greet(goal[RIGHT], c))
 
     k_copy = pltpu.make_async_copy(k_hbm, k, local_sem.at[0])
@@ -66,7 +65,7 @@
     for copy in (k_copy, row_copy, orb_copy, vec_copy):
         copy.start()
 
-    pl.semaphore_wait(barrier, nc - 1 + 2 + has_left.astype(jnp.int32) + has_right.astype(jnp.int32))
+    pl.semaphore_wait(barrier, nc - 1 + 1 - core + pair + has_left.astype(jnp.int32))
 
     def row_chunk(j, i):
         at_rows = pl.ds(i * chunk, chunk) if isinstance(i, int) else pl.ds(pl.multiple_of(i * chunk, chunk), chunk)
@@ -83,6 +82,13 @@
         for j in range(1, nc):
             row_chunk(j, i).start()
 
+    def answer(way, slot):
+        pl.semaphore_signal(ready.at[slot], inc=1, device_id=(goal[way], c), device_id_type=MESH)
+
+    pl.when(core == 0)(lambda: answer(CORE, CORE))
+    pl.when(pair == 1)(lambda: answer(PAIR, PAIR))
+    pl.when(has_left)(lambda: answer(LEFT, RIGHT))
+
     def shard(t, l, p, way, first=False):
         there = (orb, vec)[t].at[pl.ds(pl.multiple_of(at(l, p, core) * per, per), per)]
         return pltpu.make_async_remote_copy(
@@ -96,7 +102,7 @@
 
     def line_sources(d):
         if d == 0:
-            return [(line, None, ((LEFT, has_left), (RIGHT, has_right), (PAIR, None), (CORE, None)))]
+            return [(line, None, ())]
         return [
             (line - d, line - d >= 0, ((RIGHT, has_right), (PAIR, None), (CORE, None))),
             (line + d, line + d < lines, ((LEFT, has_left), (PAIR, None), (CORE, None))),
@@ -118,12 +124,10 @@
     def pass_on(t, d):
         for l, there, ways in line_sources(d):
             def go(l=l, ways=ways):
-                if d > 0:
-                    shard(t, l, pair, PAIR).wait_recv()
+                shard(t, l, pair, PAIR).wait_recv()
                 for way, cond in ways:
-                    when(cond, shard(t, l, pair, way, d == 0).start)
-                if d > 0:
-                    keep(t, at(l, pair, core))
+                    when(cond, shard(t, l, pair, way).start)
+                keep(t, at(l, pair, core))
             when(there, go)
 
     def pass_over(t, d):
@@ -134,9 +138,20 @@
                 keep(t, at(l, 1 - pair, core))
             when(there, go)
 
+    behind = ((CORE, core == 1), (PAIR, pair == 0), (RIGHT, has_right))
+    for t in range(2):
+        for way, cond in ((LEFT, has_left), (PAIR, pair == 1), (CORE, core == 0)):
+            pl.when(cond)(shard(t, line, pair, way, True).start)
+    for way, cond in behind:
+        pl.when(cond)(lambda way=way: pl.semaphore_wait(ready.at[way], 1))
+    for t in range(2):
+        for way, cond in behind:
+            pl.when(cond)(shard(t, line, pair, way, True).start)
+
     for d in range(lines):
-        for t in range(2):
-            pass_on(t, d)
+        if d > 0:
+            for t in range(2):
+                pass_on(t, d)
         if d > 0:
             for t in range(2):
                 pass_over(t, d - 1)
@@ -248,6 +263,7 @@
                 pltpu.VMEM((nc - 1, chunks, nb, chunk), f32),
                 pltpu.VMEM((chunks, nb, chunk), f32),
                 dma((4,)),
+                pltpu.SemaphoreType.REGULAR((4,)),
                 dma((nc - 1,)),
                 dma((nc - 1, chunks)),
                 dma((4,)),

time: 51.1 us -> 51 us (level)
  no operation moved by 1% of the time
where the time goes in v1:
time: 51 us; the launch traced here: 50.8 us
  Pallas kernels  49.9 us (98%)
  local copies, waits for them, and re-layouts  0.97 us (2%)
    pallas_call x1, Pallas kernels, body(): pl.pallas_call(functools.partial(exchange_kernel, nr, nc, chunks), out_sh...  49.9 us

profile of v1, /device:TPU:0, one launch (start us, length us, event | category | flops | bytes accessed | tf_op | source)
XLA Modules:
  0.0 50.8 jit_solution(14717743034843193106)
XLA Ops:
  0.0 49.9 %shard_map.46 = f32[256,1024]{1,0:T(8,128)S(1)} custom-call(f32[1024,768]{1,0:T(8,128)} %k_hbm.1, f32[1024,256]{1,0:T(8,128)} %row_hbm.1, f32[32,768]{1,0:T(8,128)} %bitcast.2, f32[32,768]{1,0:T(8,128)} %bitcast.3), custom_call_target="tpu_custom_call" | custom-call | tf_op jit(solution)/shard_map/pallas_call | solution.py:248
  49.9 1.0 %copy.6 = f32[256,1024]{1,0:T(8,128)} copy(f32[256,1024]{1,0:T(8,128)S(1)} %shard_map.46) | data formatting | bytes 2097152

commit v2 on v1

--- a/solution.py
+++ b/solution.py
@@ -22,9 +22,9 @@
 
 
 def exchange_kernel(
-    nr, nc, chunks,
+    nr, nc, chunks, pieces,
     k_hbm, row_hbm, orb_hbm, vec_hbm, out_ref,
-    k, rows, orb, vec, orb_hi, orb_lo, vec_hi, vec_lo, theirs, got, mine,
+    k, rows, orb, vec, orb_hi, orb_lo, vec_hi, vec_lo, w_hi, w_lo, theirs, got,
     local_sem, ready, row_send, row_recv, col_send, col_recv, core_recv, out_send, out_recv,
 ):
     r, c = lax.axis_index("rows"), lax.axis_index("cols")
@@ -89,16 +89,30 @@
     pl.when(pair == 1)(lambda: answer(PAIR, PAIR))
     pl.when(has_left)(lambda: answer(LEFT, RIGHT))
 
-    def shard(t, l, p, way, first=False):
-        there = (orb, vec)[t].at[pl.ds(pl.multiple_of(at(l, p, core) * per, per), per)]
+    split_by = pieces // 2
+    part = per // split_by
+    late_lines = lines // nc if lines % nc == 0 else 0
+
+    def late(l):
+        return l // late_lines == c if late_lines else l < 0
+
+    def at_piece(q, s):
+        return pl.ds(pl.multiple_of(s * per + q % split_by * part, part), part)
+
+    def shard(q, l, p, way, first=False):
+        t = q // split_by
+        there = (orb, vec)[t].at[at_piece(q, at(l, p, core))]
         return pltpu.make_async_remote_copy(
-            src_ref=(orb_hbm, vec_hbm)[t] if first else there,
+            src_ref=(orb_hbm, vec_hbm)[t].at[pl.ds(q % split_by * part, part)] if first else there,
             dst_ref=there,
             send_sem=col_send.at[way],
-            recv_sem=core_recv.at[0] if way == CORE else col_recv.at[t, p, l],
+            recv_sem=core_recv.at[phase_of(q, l)] if way == CORE else col_recv.at[q, p, l],
             device_id=(goal[way], c),
             device_id_type=MESH,
         )
+
+    def phase_of(q, l):
+        return 0 if q < split_by else late(l).astype(jnp.int32)
 
     def line_sources(d):
         if d == 0:
@@ -108,63 +122,75 @@
             (line + d, line + d < lines, ((LEFT, has_left), (PAIR, None), (CORE, None))),
         ]
 
+    def both(a, b):
+        return b if a is None else a if b is None else a & b
+
     def when(cond, do):
         if cond is None:
             do()
         else:
             pl.when(cond)(do)
 
-    def keep(t, s):
-        here = pl.ds(pl.multiple_of(s * per, per), per)
+    def keep(t, rows_here):
         if t == 0:
-            orb_hi[here], orb_lo[here] = split(orb[here])
+            orb_hi[rows_here], orb_lo[rows_here] = split(orb[rows_here])
         else:
-            vec_hi[here], vec_lo[here] = split(-vec[here])
-
-    def pass_on(t, d):
+            vec_hi[rows_here], vec_lo[rows_here] = split(-vec[rows_here])
+
+    def whole(s):
+        return pl.ds(pl.multiple_of(s * per, per), per)
+
+    def now(q, l, second):
+        if q < split_by:
+            return None
+        return late(l) if second else ~late(l)
+
+    def pass_on(q, d, second):
         for l, there, ways in line_sources(d):
             def go(l=l, ways=ways):
-                shard(t, l, pair, PAIR).wait_recv()
+                shard(q, l, pair, PAIR).wait_recv()
                 for way, cond in ways:
-                    when(cond, shard(t, l, pair, way).start)
-                keep(t, at(l, pair, core))
-            when(there, go)
-
-    def pass_over(t, d):
+                    when(cond, shard(q, l, pair, way).start)
+                keep(q // split_by, at_piece(q, at(l, pair, core)))
+            when(both(there, now(q, l, second)), go)
+
+    def pass_over(q, d, second):
         for l, there, _ in line_sources(d):
             def go(l=l):
-                shard(t, l, 1 - pair, PAIR).wait_recv()
-                shard(t, l, 1 - pair, CORE).start()
-                keep(t, at(l, 1 - pair, core))
-            when(there, go)
-
+                shard(q, l, 1 - pair, PAIR).wait_recv()
+                shard(q, l, 1 - pair, CORE).start()
+                keep(q // split_by, at_piece(q, at(l, 1 - pair, core)))
+            when(both(there, now(q, l, second)), go)
+
+    def gather(some, second):
+        for d in range(1, lines):
+            for q in some:
+                pass_on(q, d, second)
+            for q in some:
+                pass_over(q, d - 1, second)
+        for q in some:
+            pass_over(q, lines - 1, second)
+
+    ahead = ((LEFT, has_left), (PAIR, pair == 1), (CORE, core == 0))
     behind = ((CORE, core == 1), (PAIR, pair == 0), (RIGHT, has_right))
-    for t in range(2):
-        for way, cond in ((LEFT, has_left), (PAIR, pair == 1), (CORE, core == 0)):
-            pl.when(cond)(shard(t, line, pair, way, True).start)
+    for q in range(pieces):
+        for way, cond in ahead:
+            when(both(cond, now(q, line, False)), shard(q, line, pair, way, True).start)
     for way, cond in behind:
         pl.when(cond)(lambda way=way: pl.semaphore_wait(ready.at[way], 1))
-    for t in range(2):
+    for q in range(pieces):
         for way, cond in behind:
-            pl.when(cond)(shard(t, line, pair, way, True).start)
-
-    for d in range(lines):
-        if d > 0:
-            for t in range(2):
-                pass_on(t, d)
-        if d > 0:
-            for t in range(2):
-                pass_over(t, d - 1)
-    for t in range(2):
-        pass_over(t, lines - 1)
-
-    def bulk(way, count):
-        part = orb.at[pl.ds(0, count * per)]
+            when(both(cond, now(q, line, False)), shard(q, line, pair, way, True).start)
+
+    gather(range(pieces), False)
+
+    def bulk(way, count, phase=0):
+        some = orb.at[pl.ds(0, count * per)]
         return pltpu.make_async_remote_copy(
-            src_ref=part,
-            dst_ref=part,
+            src_ref=some,
+            dst_ref=some,
             send_sem=col_send.at[way],
-            recv_sem=core_recv.at[0],
+            recv_sem=core_recv.at[phase],
             device_id=(goal[CORE], c),
             device_id_type=MESH,
         )
@@ -172,13 +198,17 @@
     for copy in (orb_copy, vec_copy, k_copy, row_copy):
         copy.wait()
     for t in range(2):
-        keep(t, r)
-    bulk(CORE, nr).wait_recv()
-    for t in range(2):
-
-        @pl.loop(0, nr // 2)
-        def _(m, t=t):
-            keep(t, m * 2 + 1 - core)
+        keep(t, whole(r))
+    bulk(CORE, nr - 2 * late_lines).wait_recv()
+
+    @pl.loop(0, nr // 2)
+    def _(m):
+        keep(0, whole(m * 2 + 1 - core))
+
+    @pl.loop(0, nr // 2 - 2 * late_lines)
+    def _(m):
+        m = m + jnp.where(m >= c * 2 * late_lines, 2 * late_lines, 0)
+        keep(1, whole(m * 2 + 1 - core))
 
     def out_chunk(j, i):
         return pltpu.make_async_remote_copy(
@@ -189,6 +219,10 @@
             device_id=(r, lax.rem(c + j, nc)),
             device_id_type=MESH,
         )
+
+    def partial(j, here):
+        block = pl.ds(pl.multiple_of(lax.rem(c + j, nc) * nb, nb), nb)
+        return dot3(vec_hi[block], vec_lo[block], w_hi[here], w_lo[here], ((1,), (1,)))
 
     @pl.loop(0, chunks)
     def _(i):
@@ -200,15 +234,26 @@
             block = pl.ds(pl.multiple_of(lax.rem(c - j + nc, nc) * mb, mb), mb)
             term = dot3(*split(rows[j, here, :]), orb_hi[block], orb_lo[block], ((1,), (0,)))
             gram = term if gram is None else gram + term
-        w_hi, w_lo = split(k[here] * gram)
-        for j in list(range(1, nc)) + [0]:
-            block = pl.ds(pl.multiple_of(lax.rem(c + j, nc) * nb, nb), nb)
-            part = dot3(vec_hi[block], vec_lo[block], w_hi, w_lo, ((1,), (1,)))
-            if j == 0:
-                mine[i] = part
-            else:
-                theirs[j - 1, i] = part
-                out_chunk(j, i).start()
+        w_hi[here], w_lo[here] = split(k[here] * gram)
+        for j in range(1, nc):
+            theirs[j - 1, i] = partial(j, here)
+            out_chunk(j, i).start()
+
+    if late_lines:
+        for way, cond in ahead + behind:
+            for q in range(split_by, pieces):
+                pl.when(cond & late(line))(shard(q, line, pair, way, True).start)
+        gather(range(split_by, pieces), True)
+        bulk(CORE, 2 * late_lines, 1).wait_recv()
+
+        @pl.loop(0, 2 * late_lines)
+        def _(m):
+            keep(1, whole((c * 2 * late_lines + m) * 2 + 1 - core))
+
+    @pl.loop(0, chunks)
+    def _(i):
+        here = pl.ds(pl.multiple_of(i * chunk, chunk), chunk)
+        out_ref[:, here] = partial(0, here)
 
     bulk(PAIR, 2 * lines).wait_send()
     bulk(CORE, nr).wait_send()
@@ -219,11 +264,12 @@
             pl.when(line == l)(bulk(RIGHT, 2 * (l + 1)).wait_send)
 
     for i in range(chunks):
-        total = mine[i]
+        here = pl.ds(i * chunk, chunk)
+        total = out_ref[:, here]
         for j in range(1, nc):
             out_chunk(j, i).wait_recv()
             total = total + got[j - 1, i]
-        out_ref[:, i * chunk:(i + 1) * chunk] = total
+        out_ref[:, here] = total
     for j in range(1, nc):
         peer = {"device_id": (r, lax.rem(c + j, nc)), "device_id_type": MESH}
         pltpu.make_async_remote_copy(
@@ -244,9 +290,10 @@
         nb = norb // nc
         chunks = n_rows // 256
         chunk = n_rows // chunks
+        pieces = 4 if per % 32 == 0 else 2
         f32, bf16, dma = jnp.float32, jnp.bfloat16, pltpu.SemaphoreType.DMA
         return pl.pallas_call(
-            functools.partial(exchange_kernel, nr, nc, chunks),
+            functools.partial(exchange_kernel, nr, nc, chunks, pieces),
             out_shape=pltpu.VMEM((nb, n_rows), f32),
             in_specs=[pl.BlockSpec(memory_space=pl.ANY)] * 4,
             out_specs=pl.BlockSpec(memory_space=pltpu.VMEM),
@@ -259,16 +306,17 @@
                 pltpu.VMEM((norb, n_cols), bf16),
                 pltpu.VMEM((norb, n_cols), bf16),
                 pltpu.VMEM((norb, n_cols), bf16),
+                pltpu.VMEM((n_rows, n_cols), bf16),
+                pltpu.VMEM((n_rows, n_cols), bf16),
                 pltpu.VMEM((nc - 1, chunks, nb, chunk), f32),
                 pltpu.VMEM((nc - 1, chunks, nb, chunk), f32),
-                pltpu.VMEM((chunks, nb, chunk), f32),
                 dma((4,)),
                 pltpu.SemaphoreType.REGULAR((4,)),
                 dma((nc - 1,)),
                 dma((nc - 1, chunks)),
                 dma((4,)),
-                dma((2, 2, nr // 4)),
-                dma((1,)),
+                dma((pieces, 2, nr // 4)),
+                dma((2,)),
                 dma((nc - 1,)),
                 dma((nc - 1, chunks)),
             ],

time: 51 us -> 50.5 us (level)
  no operation moved by 1% of the time
where the time goes in v2:
time: 50.5 us; the launch traced here: 50.4 us
  Pallas kernels  49.4 us (98%)
  local copies, waits for them, and re-layouts  0.97 us (2%)
    pallas_call x1, Pallas kernels, body(): pl.pallas_call(functools.partial(exchange_kernel, nr, nc, chunks, pieces)...  49.4 us

profile of v2, /device:TPU:0, one launch (start us, length us, event | category | flops | bytes accessed | tf_op | source)
XLA Modules:
  0.0 50.4 jit_solution(1780520124103010497)
XLA Ops:
  0.0 49.4 %shard_map.46 = f32[256,1024]{1,0:T(8,128)S(1)} custom-call(f32[1024,768]{1,0:T(8,128)} %k_hbm.1, f32[1024,256]{1,0:T(8,128)} %row_hbm.1, f32[32,768]{1,0:T(8,128)} %bitcast.2, f32[32,768]{1,0:T(8,128)} %bitcast.3), custom_call_target="tpu_custom_call" | custom-call | tf_op jit(solution)/shard_map/pallas_call | solution.py:295
  49.4 1.0 %copy.6 = f32[256,1024]{1,0:T(8,128)} copy(f32[256,1024]{1,0:T(8,128)S(1)} %shard_map.46) | data formatting | bytes 2097152

commit v3 on v2

--- a/solution.py
+++ b/solution.py
@@ -22,10 +22,10 @@
 
 
 def exchange_kernel(
-    nr, nc, chunks, pieces,
+    nr, nc, chunks, pieces, detour,
     k_hbm, row_hbm, orb_hbm, vec_hbm, out_ref,
-    k, rows, orb, vec, orb_hi, orb_lo, vec_hi, vec_lo, w_hi, w_lo, theirs, got,
-    local_sem, ready, row_send, row_recv, col_send, col_recv, core_recv, out_send, out_recv,
+    k, rows, orb, vec, orb_hi, orb_lo, vec_hi, vec_lo, w_hi, w_lo, theirs, got, relay,
+    local_sem, ready, row_send, row_recv, col_send, col_recv, core_recv, out_send, out_recv, relay_send, relay_recv,
 ):
     r, c = lax.axis_index("rows"), lax.axis_index("cols")
     core, chip = lax.rem(r, 2), r // 2
@@ -62,13 +62,11 @@
     own = pl.ds(pl.multiple_of(r * per, per), per)
     orb_copy = pltpu.make_async_copy(orb_hbm, orb.at[own], local_sem.at[2])
     vec_copy = pltpu.make_async_copy(vec_hbm, vec.at[own], local_sem.at[3])
-    for copy in (k_copy, row_copy, orb_copy, vec_copy):
-        copy.start()
 
     pl.semaphore_wait(barrier, nc - 1 + 1 - core + pair + has_left.astype(jnp.int32))
 
-    def row_chunk(j, i):
-        at_rows = pl.ds(i * chunk, chunk) if isinstance(i, int) else pl.ds(pl.multiple_of(i * chunk, chunk), chunk)
+    def row_chunk(j, i, size=chunk):
+        at_rows = pl.ds(i * chunk if isinstance(i, int) else pl.multiple_of(i * chunk, chunk), size)
         return pltpu.make_async_remote_copy(
             src_ref=row_hbm.at[at_rows],
             dst_ref=rows.at[j, at_rows],
@@ -78,9 +76,28 @@
             device_id_type=MESH,
         )
 
+    to_first = (r == 0) & (c == 1)
+    helps = [(at(0, 1, 0), PAIR), (at(1, 0, 0), RIGHT)] if detour else []
+    direct = chunk - len(helps) * detour
+
+    def row_tail(h, device, src=row_hbm, dst=rows, send=None, recv=None):
+        there = pl.ds((chunks - 1) * chunk + direct + h * detour, detour)
+        return pltpu.make_async_remote_copy(
+            src_ref=relay if src is relay else src.at[there],
+            dst_ref=relay if dst is relay else dst.at[1, there],
+            send_sem=send,
+            recv_sem=recv,
+            device_id=device,
+            device_id_type=MESH,
+        )
+
     for i in range(chunks):
         for j in range(1, nc):
-            row_chunk(j, i).start()
+            if helps and i == chunks - 1:
+                pl.when(~to_first)(row_chunk(j, i).start)
+                pl.when(to_first)(row_chunk(j, i, direct).start)
+            else:
+                row_chunk(j, i).start()
 
     def answer(way, slot):
         pl.semaphore_signal(ready.at[slot], inc=1, device_id=(goal[way], c), device_id_type=MESH)
@@ -181,6 +198,18 @@
     for q in range(pieces):
         for way, cond in behind:
             when(both(cond, now(q, line, False)), shard(q, line, pair, way, True).start)
+
+    for h, (_, way) in enumerate(helps):
+        pl.when(to_first)(row_tail(h, (goal[way], c), row_hbm, relay, row_send.at[0], relay_recv.at[0]).start)
+    for h, (helper, _) in enumerate(helps):
+
+        @pl.when((r == helper) & (c == 1))
+        def _(h=h):
+            row_tail(h, (r, 0), row_hbm, relay, relay_send.at[0], relay_recv.at[0]).wait_recv()
+            row_tail(h, (r, 0), relay, relay, relay_send.at[0], relay_recv.at[0]).start()
+
+    for copy in (k_copy, row_copy, orb_copy, vec_copy):
+        copy.start()
 
     gather(range(pieces), False)
 
@@ -239,6 +268,13 @@
             theirs[j - 1, i] = partial(j, here)
             out_chunk(j, i).start()
 
+    for h, (helper, _) in enumerate(helps):
+
+        @pl.when((r == helper) & (c == 0))
+        def _(h=h):
+            row_tail(h, (r, 0), row_hbm, relay, relay_send.at[0], relay_recv.at[0]).wait_recv()
+            row_tail(h, (0, 0), relay, rows, relay_send.at[0], row_recv.at[0, chunks - 1]).start()
+
     if late_lines:
         for way, cond in ahead + behind:
             for q in range(split_by, pieces):
@@ -255,6 +291,8 @@
         here = pl.ds(pl.multiple_of(i * chunk, chunk), chunk)
         out_ref[:, here] = partial(0, here)
 
+    for h, (helper, _) in enumerate(helps):
+        pl.when(r == helper)(row_tail(h, (r, 0), relay, relay, relay_send.at[0], relay_recv.at[0]).wait_send)
     bulk(PAIR, 2 * lines).wait_send()
     bulk(CORE, nr).wait_send()
     for l in range(lines):
@@ -291,9 +329,10 @@
         chunks = n_rows // 256
         chunk = n_rows // chunks
         pieces = 4 if per % 32 == 0 else 2
+        detour = n_rows // 1024 * 40 if nc == 2 and nr > 4 else 0
         f32, bf16, dma = jnp.float32, jnp.bfloat16, pltpu.SemaphoreType.DMA
         return pl.pallas_call(
-            functools.partial(exchange_kernel, nr, nc, chunks, pieces),
+            functools.partial(exchange_kernel, nr, nc, chunks, pieces, detour),
             out_shape=pltpu.VMEM((nb, n_rows), f32),
             in_specs=[pl.BlockSpec(memory_space=pl.ANY)] * 4,
             out_specs=pl.BlockSpec(memory_space=pltpu.VMEM),
@@ -310,6 +349,7 @@
                 pltpu.VMEM((n_rows, n_cols), bf16),
                 pltpu.VMEM((nc - 1, chunks, nb, chunk), f32),
                 pltpu.VMEM((nc - 1, chunks, nb, chunk), f32),
+                pltpu.VMEM((max(detour, 8), mb), f32),
                 dma((4,)),
                 pltpu.SemaphoreType.REGULAR((4,)),
                 dma((nc - 1,)),
@@ -319,6 +359,8 @@
                 dma((2,)),
                 dma((nc - 1,)),
                 dma((nc - 1, chunks)),
+                dma((1,)),
+                dma((1,)),
             ],
             compiler_params=pltpu.CompilerParams(
                 collective_id=0, has_side_effects=True, vmem_limit_bytes=60 * 1024 * 1024

time: 50.5 us -> 49.7 us (0.984)
  Pallas kernels: 49.4 us -> 48.6 us
    pallas_call x1, Pallas kernels: 49.4 us -> 48.6 us  [body(): pl.pallas_call(functools.partial(exchange_kernel, nr, nc, chunks, pieces,...]
where the time goes in v3:
time: 49.7 us; the launch traced here: 49.6 us
  Pallas kernels  48.6 us (98%)
  local copies, waits for them, and re-layouts  0.97 us (2%)
    pallas_call x1, Pallas kernels, body(): pl.pallas_call(functools.partial(exchange_kernel, nr, nc, chunks, pieces,...  48.6 us

profile of v3, /device:TPU:0, one launch (start us, length us, event | category | flops | bytes accessed | tf_op | source)
XLA Modules:
  0.0 49.6 jit_solution(13826361635979883990)
XLA Ops:
  0.0 48.6 %shard_map.46 = f32[256,1024]{1,0:T(8,128)S(1)} custom-call(f32[1024,768]{1,0:T(8,128)} %k_hbm.1, f32[1024,256]{1,0:T(8,128)} %row_hbm.1, f32[32,768]{1,0:T(8,128)} %bitcast.2, f32[32,768]{1,0:T(8,128)} %bitcast.3), custom_call_target="tpu_custom_call" | custom-call | tf_op jit(solution)/shard_map/pallas_call | solution.py:334
  48.6 1.0 %copy.6 = f32[256,1024]{1,0:T(8,128)} copy(f32[256,1024]{1,0:T(8,128)S(1)} %shard_map.46) | data formatting | bytes 2097152

commit v4 on v3

--- a/solution.py
+++ b/solution.py
@@ -22,7 +22,7 @@
 
 
 def exchange_kernel(
-    nr, nc, chunks, pieces, detour,
+    nr, nc, chunks, pieces, helpers, detour,
     k_hbm, row_hbm, orb_hbm, vec_hbm, out_ref,
     k, rows, orb, vec, orb_hi, orb_lo, vec_hi, vec_lo, w_hi, w_lo, theirs, got, relay,
     local_sem, ready, row_send, row_recv, col_send, col_recv, core_recv, out_send, out_recv, relay_send, relay_recv,
@@ -77,11 +77,11 @@
         )
 
     to_first = (r == 0) & (c == 1)
-    helps = [(at(0, 1, 0), PAIR), (at(1, 0, 0), RIGHT)] if detour else []
-    direct = chunk - len(helps) * detour
-
-    def row_tail(h, device, src=row_hbm, dst=rows, send=None, recv=None):
-        there = pl.ds((chunks - 1) * chunk + direct + h * detour, detour)
+    helper = (core == 0) & (chip > 0) & (chip <= helpers)
+    direct = chunk - helpers * detour
+
+    def row_tail(h, device, src, dst, send, recv):
+        there = pl.ds(pl.multiple_of((chunks - 1) * chunk + direct + h * detour, 8), detour)
         return pltpu.make_async_remote_copy(
             src_ref=relay if src is relay else src.at[there],
             dst_ref=relay if dst is relay else dst.at[1, there],
@@ -91,9 +91,18 @@
             device_id_type=MESH,
         )
 
+    def row_across():
+        return row_tail(0, (r, 0), relay, relay, relay_send.at[0], relay_recv.at[0])
+
+    def row_round(l, p):
+        h = l * 2 + p - 1
+        if h < helpers:
+            to = (at(l, p, 0), c)
+            pl.when(to_first)(row_tail(h, to, row_hbm, relay, row_send.at[0], relay_recv.at[0]).start)
+
     for i in range(chunks):
         for j in range(1, nc):
-            if helps and i == chunks - 1:
+            if helpers and i == chunks - 1:
                 pl.when(~to_first)(row_chunk(j, i).start)
                 pl.when(to_first)(row_chunk(j, i, direct).start)
             else:
@@ -179,12 +188,13 @@
                 keep(q // split_by, at_piece(q, at(l, 1 - pair, core)))
             when(both(there, now(q, l, second)), go)
 
-    def gather(some, second):
+    def gather(some, second, after=lambda d: None):
         for d in range(1, lines):
             for q in some:
                 pass_on(q, d, second)
             for q in some:
                 pass_over(q, d - 1, second)
+            after(d)
         for q in some:
             pass_over(q, lines - 1, second)
 
@@ -199,19 +209,17 @@
         for way, cond in behind:
             when(both(cond, now(q, line, False)), shard(q, line, pair, way, True).start)
 
-    for h, (_, way) in enumerate(helps):
-        pl.when(to_first)(row_tail(h, (goal[way], c), row_hbm, relay, row_send.at[0], relay_recv.at[0]).start)
-    for h, (helper, _) in enumerate(helps):
-
-        @pl.when((r == helper) & (c == 1))
-        def _(h=h):
-            row_tail(h, (r, 0), row_hbm, relay, relay_send.at[0], relay_recv.at[0]).wait_recv()
-            row_tail(h, (r, 0), relay, relay, relay_send.at[0], relay_recv.at[0]).start()
-
+    row_round(0, 1)
+    row_round(1, 0)
     for copy in (k_copy, row_copy, orb_copy, vec_copy):
         copy.start()
-
-    gather(range(pieces), False)
+    gather(range(pieces), False, lambda d: (row_round(d, 0), row_round(d - 1, 1)) if d > 1 else None)
+    if helpers:
+
+        @pl.when(helper & (c == 1))
+        def _():
+            row_across().wait_recv()
+            row_across().start()
 
     def bulk(way, count, phase=0):
         some = orb.at[pl.ds(0, count * per)]
@@ -268,17 +276,19 @@
             theirs[j - 1, i] = partial(j, here)
             out_chunk(j, i).start()
 
-    for h, (helper, _) in enumerate(helps):
-
-        @pl.when((r == helper) & (c == 0))
-        def _(h=h):
-            row_tail(h, (r, 0), row_hbm, relay, relay_send.at[0], relay_recv.at[0]).wait_recv()
-            row_tail(h, (0, 0), relay, rows, relay_send.at[0], row_recv.at[0, chunks - 1]).start()
+        if late_lines:
+            for way, cond in ahead + behind:
+                for q in range(split_by, pieces):
+                    pl.when(cond & late(line) & (i == 0))(shard(q, line, pair, way, True).start)
+
+    if helpers:
+
+        @pl.when(helper & (c == 0))
+        def _():
+            row_across().wait_recv()
+            row_tail(chip - 1, (0, 0), relay, rows, relay_send.at[0], row_recv.at[0, chunks - 1]).start()
 
     if late_lines:
-        for way, cond in ahead + behind:
-            for q in range(split_by, pieces):
-                pl.when(cond & late(line))(shard(q, line, pair, way, True).start)
         gather(range(split_by, pieces), True)
         bulk(CORE, 2 * late_lines, 1).wait_recv()
 
@@ -291,8 +301,8 @@
         here = pl.ds(pl.multiple_of(i * chunk, chunk), chunk)
         out_ref[:, here] = partial(0, here)
 
-    for h, (helper, _) in enumerate(helps):
-        pl.when(r == helper)(row_tail(h, (r, 0), relay, relay, relay_send.at[0], relay_recv.at[0]).wait_send)
+    if helpers:
+        pl.when(helper)(row_across().wait_send)
     bulk(PAIR, 2 * lines).wait_send()
     bulk(CORE, nr).wait_send()
     for l in range(lines):
@@ -329,10 +339,11 @@
         chunks = n_rows // 256
         chunk = n_rows // chunks
         pieces = 4 if per % 32 == 0 else 2
-        detour = n_rows // 1024 * 40 if nc == 2 and nr > 4 else 0
+        helpers = min(nr // 2 - 2, 6) if nc == 2 else 0
+        detour = n_rows // 64
         f32, bf16, dma = jnp.float32, jnp.bfloat16, pltpu.SemaphoreType.DMA
         return pl.pallas_call(
-            functools.partial(exchange_kernel, nr, nc, chunks, pieces, detour),
+            functools.partial(exchange_kernel, nr, nc, chunks, pieces, helpers, detour),
             out_shape=pltpu.VMEM((nb, n_rows), f32),
             in_specs=[pl.BlockSpec(memory_space=pl.ANY)] * 4,
             out_specs=pl.BlockSpec(memory_space=pltpu.VMEM),
@@ -349,7 +360,7 @@
                 pltpu.VMEM((n_rows, n_cols), bf16),
                 pltpu.VMEM((nc - 1, chunks, nb, chunk), f32),
                 pltpu.VMEM((nc - 1, chunks, nb, chunk), f32),
-                pltpu.VMEM((max(detour, 8), mb), f32),
+                pltpu.VMEM((detour, mb), f32),
                 dma((4,)),
                 pltpu.SemaphoreType.REGULAR((4,)),
                 dma((nc - 1,)),

time: 49.7 us -> 49.7 us (level)
  no operation moved by 1% of the time
where the time goes in v4:
time: 49.7 us; the launch traced here: 49.6 us
  Pallas kernels  48.6 us (98%)
  local copies, waits for them, and re-layouts  0.97 us (2%)
    pallas_call x1, Pallas kernels, body(): pl.pallas_call(functools.partial(exchange_kernel, nr, nc, chunks, pieces,...  48.6 us

profile of v4, /device:TPU:0, one launch (start us, length us, event | category | flops | bytes accessed | tf_op | source)
XLA Modules:
  0.0 49.6 jit_solution(17605026241235384622)
XLA Ops:
  0.0 48.6 %shard_map.46 = f32[256,1024]{1,0:T(8,128)S(1)} custom-call(f32[1024,768]{1,0:T(8,128)} %k_hbm.1, f32[1024,256]{1,0:T(8,128)} %row_hbm.1, f32[32,768]{1,0:T(8,128)} %bitcast.2, f32[32,768]{1,0:T(8,128)} %bitcast.3), custom_call_target="tpu_custom_call" | custom-call | tf_op jit(solution)/shard_map/pallas_call | solution.py:345
  48.6 1.0 %copy.6 = f32[256,1024]{1,0:T(8,128)} copy(f32[256,1024]{1,0:T(8,128)S(1)} %shard_map.46) | data formatting | bytes 2097152

commit v5 on v4

--- a/solution.py
+++ b/solution.py
@@ -76,35 +76,32 @@
             device_id_type=MESH,
         )
 
-    to_first = (r == 0) & (c == 1)
+    first = r == 0
     helper = (core == 0) & (chip > 0) & (chip <= helpers)
     direct = chunk - helpers * detour
-
-    def row_tail(h, device, src, dst, send, recv):
+    TO, ACROSS, BACK = range(3)
+
+    def row_round(leg, h, device):
         there = pl.ds(pl.multiple_of((chunks - 1) * chunk + direct + h * detour, 8), detour)
         return pltpu.make_async_remote_copy(
-            src_ref=relay if src is relay else src.at[there],
-            dst_ref=relay if dst is relay else dst.at[1, there],
-            send_sem=send,
-            recv_sem=recv,
+            src_ref=row_hbm.at[there] if leg == TO else relay.at[leg - 1],
+            dst_ref=rows.at[1, there] if leg == BACK else relay.at[leg],
+            send_sem=row_send.at[0] if leg == TO else relay_send.at[leg - 1],
+            recv_sem=row_recv.at[0, chunks - 1] if leg == BACK else relay_recv.at[leg],
             device_id=device,
             device_id_type=MESH,
         )
 
-    def row_across():
-        return row_tail(0, (r, 0), relay, relay, relay_send.at[0], relay_recv.at[0])
-
-    def row_round(l, p):
+    def row_out(l, p):
         h = l * 2 + p - 1
         if h < helpers:
-            to = (at(l, p, 0), c)
-            pl.when(to_first)(row_tail(h, to, row_hbm, relay, row_send.at[0], relay_recv.at[0]).start)
+            pl.when(first)(row_round(TO, h, (at(l, p, 0), c)).start)
 
     for i in range(chunks):
         for j in range(1, nc):
             if helpers and i == chunks - 1:
-                pl.when(~to_first)(row_chunk(j, i).start)
-                pl.when(to_first)(row_chunk(j, i, direct).start)
+                pl.when(~first)(row_chunk(j, i).start)
+                pl.when(first)(row_chunk(j, i, direct).start)
             else:
                 row_chunk(j, i).start()
 
@@ -209,17 +206,17 @@
         for way, cond in behind:
             when(both(cond, now(q, line, False)), shard(q, line, pair, way, True).start)
 
-    row_round(0, 1)
-    row_round(1, 0)
+    row_out(0, 1)
+    row_out(1, 0)
     for copy in (k_copy, row_copy, orb_copy, vec_copy):
         copy.start()
-    gather(range(pieces), False, lambda d: (row_round(d, 0), row_round(d - 1, 1)) if d > 1 else None)
+    gather(range(pieces), False, lambda d: (row_out(d, 0), row_out(d - 1, 1)) if d > 1 else None)
     if helpers:
 
-        @pl.when(helper & (c == 1))
+        @pl.when(helper)
         def _():
-            row_across().wait_recv()
-            row_across().start()
+            row_round(TO, 0, (r, 1 - c)).wait_recv()
+            row_round(ACROSS, 0, (r, 1 - c)).start()
 
     def bulk(way, count, phase=0):
         some = orb.at[pl.ds(0, count * per)]
@@ -283,10 +280,10 @@
 
     if helpers:
 
-        @pl.when(helper & (c == 0))
+        @pl.when(helper)
         def _():
-            row_across().wait_recv()
-            row_tail(chip - 1, (0, 0), relay, rows, relay_send.at[0], row_recv.at[0, chunks - 1]).start()
+            row_round(ACROSS, 0, (r, 1 - c)).wait_recv()
+            row_round(BACK, chip - 1, (0, c)).start()
 
     if late_lines:
         gather(range(split_by, pieces), True)
@@ -302,7 +299,8 @@
         out_ref[:, here] = partial(0, here)
 
     if helpers:
-        pl.when(helper)(row_across().wait_send)
+        for leg in (ACROSS, BACK):
+            pl.when(helper)(row_round(leg, chip - 1, (0, c)).wait_send)
     bulk(PAIR, 2 * lines).wait_send()
     bulk(CORE, nr).wait_send()
     for l in range(lines):
@@ -360,7 +358,7 @@
                 pltpu.VMEM((n_rows, n_cols), bf16),
                 pltpu.VMEM((nc - 1, chunks, nb, chunk), f32),
                 pltpu.VMEM((nc - 1, chunks, nb, chunk), f32),
-                pltpu.VMEM((detour, mb), f32),
+                pltpu.VMEM((2, detour, mb), f32),
                 dma((4,)),
                 pltpu.SemaphoreType.REGULAR((4,)),
                 dma((nc - 1,)),
@@ -370,8 +368,8 @@
                 dma((2,)),
                 dma((nc - 1,)),
                 dma((nc - 1, chunks)),
-                dma((1,)),
-                dma((1,)),
+                dma((2,)),
+                dma((2,)),
             ],
             compiler_params=pltpu.CompilerParams(
                 collective_id=0, has_side_effects=True, vmem_limit_bytes=60 * 1024 * 1024

time: 49.7 us -> 49.5 us (level)
  Pallas kernels: 48.6 us -> 48.1 us
where the time goes in v5:
time: 49.5 us; the launch traced here: 49.1 us
  Pallas kernels  48.1 us (97%)
  local copies, waits for them, and re-layouts  0.97 us (2%)
    pallas_call x1, Pallas kernels, body(): pl.pallas_call(functools.partial(exchange_kernel, nr, nc, chunks, pieces,...  48.1 us

profile of v5, /device:TPU:0, one launch (start us, length us, event | category | flops | bytes accessed | tf_op | source)
XLA Modules:
  0.0 49.1 jit_solution(3850905881841315028)
XLA Ops:
  0.0 48.1 %shard_map.46 = f32[256,1024]{1,0:T(8,128)S(1)} custom-call(f32[1024,768]{1,0:T(8,128)} %k_hbm.1, f32[1024,256]{1,0:T(8,128)} %row_hbm.1, f32[32,768]{1,0:T(8,128)} %bitcast.2, f32[32,768]{1,0:T(8,128)} %bitcast.3), custom_call_target="tpu_custom_call" | custom-call | tf_op jit(solution)/shard_map/pallas_call | solution.py:343
  48.1 1.0 %copy.6 = f32[256,1024]{1,0:T(8,128)} copy(f32[256,1024]{1,0:T(8,128)S(1)} %shard_map.46) | data formatting | bytes 2097152

commit v6 on v5

--- a/solution.py
+++ b/solution.py
@@ -24,7 +24,7 @@
 def exchange_kernel(
     nr, nc, chunks, pieces, helpers, detour,
     k_hbm, row_hbm, orb_hbm, vec_hbm, out_ref,
-    k, rows, orb, vec, orb_hi, orb_lo, vec_hi, vec_lo, w_hi, w_lo, theirs, got, relay,
+    k, rows, orb, vec, orb_hi, orb_lo, vec_hi, vec_lo, w_hi, w_lo, theirs, got, relay, lead,
     local_sem, ready, row_send, row_recv, col_send, col_recv, core_recv, out_send, out_recv, relay_send, relay_recv,
 ):
     r, c = lax.axis_index("rows"), lax.axis_index("cols")
@@ -63,10 +63,24 @@
     orb_copy = pltpu.make_async_copy(orb_hbm, orb.at[own], local_sem.at[2])
     vec_copy = pltpu.make_async_copy(vec_hbm, vec.at[own], local_sem.at[3])
 
+    n_lead = lead.shape[0]
+    lead_copy = pltpu.make_async_copy(row_hbm.at[pl.ds(0, n_lead)], lead, local_sem.at[4])
+    pl.when(c == 0)(lead_copy.start)
+    pl.when(c == 0)(lead_copy.wait)
     pl.semaphore_wait(barrier, nc - 1 + 1 - core + pair + has_left.astype(jnp.int32))
 
-    def row_chunk(j, i, size=chunk):
-        at_rows = pl.ds(i * chunk if isinstance(i, int) else pl.multiple_of(i * chunk, chunk), size)
+    def row_lead(j):
+        return pltpu.make_async_remote_copy(
+            src_ref=lead,
+            dst_ref=rows.at[j, pl.ds(0, n_lead)],
+            send_sem=row_send.at[j - 1],
+            recv_sem=row_recv.at[j - 1, 0],
+            device_id=(r, lax.rem(c + j, nc)),
+            device_id_type=MESH,
+        )
+
+    def row_chunk(j, i, size=chunk, skip=0):
+        at_rows = pl.ds(i * chunk + skip if isinstance(i, int) else pl.multiple_of(i * chunk, chunk), size)
         return pltpu.make_async_remote_copy(
             src_ref=row_hbm.at[at_rows],
             dst_ref=rows.at[j, at_rows],
@@ -102,6 +116,10 @@
             if helpers and i == chunks - 1:
                 pl.when(~first)(row_chunk(j, i).start)
                 pl.when(first)(row_chunk(j, i, direct).start)
+            elif i == 0:
+                pl.when(c == 0)(row_lead(j).start)
+                pl.when(c == 0)(row_chunk(j, 0, chunk - n_lead, n_lead).start)
+                pl.when(c > 0)(row_chunk(j, 0).start)
             else:
                 row_chunk(j, i).start()
 
@@ -359,7 +377,8 @@
                 pltpu.VMEM((nc - 1, chunks, nb, chunk), f32),
                 pltpu.VMEM((nc - 1, chunks, nb, chunk), f32),
                 pltpu.VMEM((2, detour, mb), f32),
-                dma((4,)),
+                pltpu.VMEM((chunk // 4, mb), f32),
+                dma((5,)),
                 pltpu.SemaphoreType.REGULAR((4,)),
                 dma((nc - 1,)),
                 dma((nc - 1, chunks)),

time: 49.5 us -> 49.5 us (level)
  no operation moved by 1% of the time
where the time goes in v6:
time: 49.5 us; the launch traced here: 49.1 us
  Pallas kernels  48.2 us (97%)
  local copies, waits for them, and re-layouts  0.97 us (2%)
    pallas_call x1, Pallas kernels, body(): pl.pallas_call(functools.partial(exchange_kernel, nr, nc, chunks, pieces,...  48.2 us

profile of v6, /device:TPU:0, one launch (start us, length us, event | category | flops | bytes accessed | tf_op | source)
XLA Modules:
  0.0 49.1 jit_solution(6386209142733093587)
XLA Ops:
  0.0 48.2 %shard_map.46 = f32[256,1024]{1,0:T(8,128)S(1)} custom-call(f32[1024,768]{1,0:T(8,128)} %k_hbm.1, f32[1024,256]{1,0:T(8,128)} %row_hbm.1, f32[32,768]{1,0:T(8,128)} %bitcast.2, f32[32,768]{1,0:T(8,128)} %bitcast.3), custom_call_target="tpu_custom_call" | custom-call | tf_op jit(solution)/shard_map/pallas_call | solution.py:361
  48.2 1.0 %copy.6 = f32[256,1024]{1,0:T(8,128)} copy(f32[256,1024]{1,0:T(8,128)S(1)} %shard_map.46) | data formatting | bytes 2097152
